TPU v7x, 512 devices: a whole 4x8x8 slice. The times are simulated.
512 devices in a mesh: dp: 32 (over x_hi, y, core), vocab: 16 (over z, x_lo).
Axes of the slice: x: 4 (x_hi: 2, x_lo: 2; x = x_hi * 2 + x_lo), y: 8, z: 8, core: 2. Of those that a mesh axis runs over, the one named last changes fastest.
Arguments:
- final_states: bfloat16 [65536, 5376], P(('dp', 'vocab')), may hold values from -12 to 12
- head_blocks: bfloat16 [16, 128, 5376], P('vocab'), may hold values from -0.17048273 to 0.17048273
- block_order: int32 [16], replicated, may hold values from 0 to 15, as said below
- row_tags: int32 [65536], P(('dp', 'vocab')), may hold values from 0 to 3, as said below
- target_word: int32 [65536], P(('dp', 'vocab')), may hold values from 0 to 511
- row_weight: bfloat16 [65536], P(('dp', 'vocab')), may hold values from 0.25 to 2
Outputs:
- row_loss: float32 [65536], P(('dp', 'vocab'))
- state_grad: bfloat16 [65536, 5376], P(('dp', 'vocab'))
- head_grad: float32 [16, 128, 5376], P('vocab', 'dp')
Inputs may be any that keep to these rules, and one draw needn't show every extreme that they name: `row_tags`: among the rows of one device at most 40 carry any one tag; one tag, the same on every device, is carried by exactly 40 rows of each device. Each block number appears once; the shortlist of tag l is block_order[l * 4] to block_order[(l + 1) * 4 - 1].
All inputs are finite; a program needn't handle non-finite values.
Results may differ from a plain program's by a relative error of at most 0.0052.
Values may be sent and summed in bfloat16 or wider, within the bound.
No kernel may reach another device: no remote copies, remote signals or barrier semaphores. Data moves between devices by JAX's collectives and lax.ppermute only.
A program may use at most 128 MiB of HBM per device.

v0:
```python
import jax
import jax.numpy as jnp
from jax import lax
from jax.sharding import PartitionSpec as P

BLOCK = 128
LANGS = 4


def shards(final_states, head_blocks, block_order, row_tags, target_word, row_weight):
    shard_count = lax.axis_size("vocab")
    rows_here = final_states.shape[0]
    short_len = shard_count // LANGS
    capacity = rows_here * 5 // 16
    block_ids = jnp.arange(shard_count, dtype=jnp.int32)
    placed = jnp.sum(
        block_ids[:, None] * (block_order[:, None] == block_ids[None, :]).astype(jnp.int32), axis=0
    )
    owner_tag = placed // short_len
    owner_slot = placed % short_len
    tag_ids = jnp.arange(LANGS, dtype=jnp.int32)
    tag_onehot = (row_tags[:, None] == tag_ids[None, :]).astype(jnp.int32)
    row_rank = jnp.sum((jnp.cumsum(tag_onehot, axis=0) - 1) * tag_onehot, axis=1)
    routed = owner_tag[:, None] == row_tags[None, :]
    slot_ids = jnp.arange(capacity, dtype=jnp.int32)
    chosen = routed[:, None, :] & (row_rank[None, None, :] == slot_ids[None, :, None])
    chosen_int = chosen.astype(jnp.int32)
    slot_used = jnp.sum(chosen_int, axis=2) > 0
    row_ids = jnp.arange(rows_here, dtype=jnp.int32)
    slot_row = jnp.sum(chosen_int * row_ids[None, None, :], axis=2)
    sent_rows = jnp.where(
        slot_used[:, :, None], jnp.take(final_states, slot_row, axis=0), jnp.zeros((), jnp.bfloat16)
    )
    local_word = jnp.where(
        target_word[None, :] // BLOCK == owner_slot[:, None], target_word[None, :] % BLOCK, -1
    )
    slot_word = jnp.sum(chosen_int * (local_word[:, None, :] + 1), axis=2) - 1
    slot_label = jnp.where(slot_used, slot_row, -1)
    slot_weight = jnp.sum(
        jnp.where(chosen, row_weight.astype(jnp.float32)[None, None, :], 0.0), axis=2
    ).astype(jnp.bfloat16)
    got_rows, got_label, got_word, got_weight = (
        lax.all_to_all(sent_rows, "vocab", split_axis=0, concat_axis=0, tiled=True),
        lax.all_to_all(slot_label, "vocab", split_axis=0, concat_axis=0, tiled=True),
        lax.all_to_all(slot_word, "vocab", split_axis=0, concat_axis=0, tiled=True),
        lax.all_to_all(slot_weight, "vocab", split_axis=0, concat_axis=0, tiled=True),
    )
    own_block = head_blocks[0]
    logits = jnp.einsum("scd,wd->scw", got_rows, own_block, preferred_element_type=jnp.float32)
    word_ids = jnp.arange(BLOCK, dtype=jnp.int32)
    target_hit = word_ids[None, None, :] == got_word[:, :, None]
    slot_peak = jnp.max(logits, axis=2)
    slot_total = jnp.sum(jnp.exp(logits - slot_peak[:, :, None]), axis=2)
    slot_picked = jnp.sum(jnp.where(target_hit, logits, 0.0), axis=2)
    back_peak, back_total, back_picked = (
        lax.all_to_all(slot_peak, "vocab", split_axis=0, concat_axis=0, tiled=True),
        lax.all_to_all(slot_total, "vocab", split_axis=0, concat_axis=0, tiled=True),
        lax.all_to_all(slot_picked, "vocab", split_axis=0, concat_axis=0, tiled=True),
    )
    row_peak = jnp.take(back_peak, row_rank, axis=1)
    row_total = jnp.take(back_total, row_rank, axis=1)
    row_picked = jnp.take(back_picked, row_rank, axis=1)
    peak_max = jnp.max(jnp.where(routed, row_peak, -1e30), axis=0)
    summed = jnp.sum(
        jnp.where(routed, row_total * jnp.exp(row_peak - peak_max[None, :]), 0.0), axis=0
    )
    log_total = peak_max + jnp.log(summed)
    row_loss = log_total - jnp.sum(jnp.where(routed, row_picked, 0.0), axis=0)
    slot_lse = jnp.where(slot_used, jnp.take(log_total, slot_row), 0.0)
    got_lse = lax.all_to_all(slot_lse, "vocab", split_axis=0, concat_axis=0, tiled=True)
    slot_probs = jnp.exp(logits - got_lse[:, :, None])
    slot_grads = (
        got_weight.astype(jnp.float32)[:, :, None] * (slot_probs - target_hit.astype(jnp.float32))
    ).astype(jnp.bfloat16)
    part_grads = jnp.einsum(
        "scw,wd->scd", slot_grads, own_block, preferred_element_type=jnp.float32
    ).astype(jnp.bfloat16)
    back_grads = lax.all_to_all(part_grads, "vocab", split_axis=0, concat_axis=0, tiled=True)
    state_grad = jnp.einsum(
        "sct,scd->td", chosen.astype(jnp.bfloat16), back_grads, preferred_element_type=jnp.float32
    ).astype(jnp.bfloat16)
    head_term = jnp.einsum("scw,scd->wd", slot_grads, got_rows, preferred_element_type=jnp.float32)
    head_share = lax.psum_scatter(head_term, "dp", scatter_dimension=0, tiled=True)
    return (row_loss, state_grad, head_share[None])


def solution(mesh):
    return jax.shard_map(
        shards,
        mesh=mesh,
        in_specs=(
            P(("dp", "vocab"), None),
            P("vocab", None, None),
            P(),
            P(("dp", "vocab")),
            P(("dp", "vocab")),
            P(("dp", "vocab")),
        ),
        out_specs=(P(("dp", "vocab")), P(("dp", "vocab"), None), P("vocab", "dp", None)),
        check_vma=False,
    )
```

profile of v0, /device:TPU:4, one launch (start us, length us, event | category | flops | bytes accessed | tf_op | source)
XLA Modules:
  0.0 613.4 jit_solution(15388917379976322116)
XLA Ops:
  7.2 0.8 select_reduce_fusion.2
  8.0 0.7 and_select_fusion.6
  8.7 0.7 fusion.16
  9.5 0.7 broadcast_compare_fusion
  10.3 0.2 reduce_window_sum.11
  10.5 0.8 select_reduce_fusion.1
  11.4 0.9 fusion.7
  12.3 0.1 reshape.283
  12.4 16.4 %gather_fusion = bf16[640,5376]{1,0:T(8,128)(2,1)} fusion(bf16[128,5376]{1,0:T(8,128)(2,1)} %param.8, s32[1024]{0:T(1024)S(1)} %pad_clamp_fusion.1), kind=kCustom, calls=%fused_computation.3 | custom fusion | bytes 13765120 | tf_op jit(solution)/shard_map/jit(_take)/gather | solution.py:32
  28.8 6.7 %select_select_fusion = bf16[16,40,5376]{2,1,0:T(8,128)(2,1)} fusion(bf16[16,40,5376]{2,1,0:T(8,128)(2,1)} %bitcast.65, pred[16,40]{1,0:T(8,128)(4,1)S(1)} %get-tuple-element.19, pred[16,40]{1,0:T(8,128)(4,1)S(1)} %get-tuple-element.20), kind=kLoop, calls=%fused_computation.9 | loop fusion | flops 6881280 | bytes 13763840 | tf_op jit(solution)/shard_map/jit(_where)/select_n | solution.py:31
  35.5 11.2 %all-to-all-start = ((bf16[16,40,5376]{2,1,0:T(8,128)(2,1)}), bf16[16,40,5376]{2,1,0:T(8,128)(2,1)}, u32[]{:S(2)}, u32[]{:S(2)}) async-start(bf16[16,40,5376]{2,1,0:T(8,128)(2,1)} %select_select_fusion), calls=%async_computation | async-start | bytes 13762560 | tf_op jit(solution)/shard_map/all_to_all | solution.py:43
  46.8 0.6 broadcast_add_fusion
  47.4 157.3 %all-to-all-done = bf16[16,40,5376]{2,1,0:T(8,128)(2,1)} async-done(((bf16[16,40,5376]{2,1,0:T(8,128)(2,1)}), bf16[16,40,5376]{2,1,0:T(8,128)(2,1)}, u32[]{:S(2)}, u32[]{:S(2)}) %all-to-all-start) | async-done | bytes 6881312 | tf_op jit(solution)/shard_map/all_to_all | solution.py:43
  204.7 6.4 %all-to-all-start.3 = ((s32[16,1,40]{2,1,0:T(1,128)}), s32[16,1,40]{2,1,0:T(1,128)S(1)}, u32[]{:S(2)}, u32[]{:S(2)}) async-start(s32[16,1,40]{2,1,0:T(1,128)} %bitcast.12), calls=%async_computation.3 | async-start | bytes 16384 | tf_op jit(solution)/shard_map/all_to_all | solution.py:45
  211.2 5.6 fusion.18
  216.8 2.8 all-to-all-done.3
  219.6 5.3 all-to-all-start.1
  224.9 1.8 select_reduce_fusion
  226.7 6.7 %all-to-all-done.1 = f32[16,1,40]{2,1,0:T(1,128)S(1)} async-done(((f32[16,1,40]{2,1,0:T(1,128)}), f32[16,1,40]{2,1,0:T(1,128)S(1)}, u32[]{:S(2)}, u32[]{:S(2)}) %all-to-all-start.1) | async-done | bytes 2592 | tf_op jit(solution)/shard_map/all_to_all | solution.py:56
  233.4 3.4 all-to-all-start.2
  236.8 0.2 fusion.8
  237.0 8.3 %all-to-all-done.2 = f32[16,1,40]{2,1,0:T(1,128)S(1)} async-done(((f32[16,1,40]{2,1,0:T(1,128)}), f32[16,1,40]{2,1,0:T(1,128)S(1)}, u32[]{:S(2)}, u32[]{:S(2)}) %all-to-all-start.2) | async-done | bytes 2592 | tf_op jit(solution)/shard_map/all_to_all | solution.py:57
  245.3 3.5 all-to-all-start.4
  248.8 0.6 copy.37
  249.4 0.1 copy.32
  249.4 0.6 gather_fusion.2
  250.1 0.1 copy.34
  250.2 0.6 gather_fusion.3
  250.8 6.3 %all-to-all-done.4 = f32[16,1,40]{2,1,0:T(1,128)S(1)} async-done(((f32[16,1,40]{2,1,0:T(1,128)}), f32[16,1,40]{2,1,0:T(1,128)S(1)}, u32[]{:S(2)}, u32[]{:S(2)}) %all-to-all-start.4) | async-done | bytes 2592 | tf_op jit(solution)/shard_map/all_to_all | solution.py:58
  257.1 3.4 all-to-all-start.5
  260.6 0.1 copy.36
  260.6 0.6 gather_fusion.4
  261.3 0.2 fusion.14
  261.5 0.2 fusion.11
  261.7 0.5 fusion.17
  262.2 4.1 gather_fusion.1
  266.3 0.1 gather.15
  266.4 0.6 copy_select_fusion
  267.1 2.0 all-to-all-done.5
  269.0 6.1 all-to-all-start.6
  275.1 8.4 %all-to-all-done.6 = f32[16,1,40]{2,1,0:T(1,128)S(1)} async-done(((f32[16,1,40]{2,1,0:T(1,128)}), f32[16,1,40]{2,1,0:T(1,128)S(1)}, u32[]{:S(2)}, u32[]{:S(2)}) %all-to-all-start.6) | async-done | bytes 2592 | tf_op jit(solution)/shard_map/all_to_all | solution.py:70
  283.6 4.9 convolution_convert_fusion
  288.5 4.7 all-to-all-start.7
  293.2 5.9 convolution_bitcast_fusion
  299.2 1.3 dynamic-slice
  301.1 298.6 %all-reduce.3.cloned.1.call-done = f32[128,5376]{1,0:T(8,128)} async-done(((f32[128,5376]{1,0:T(8,128)}), f32[128,5376]{1,0:T(8,128)}) %all-reduce.3.cloned.1.call-update) | async-done | bytes 2752528
  599.7 1.6 dynamic-slice_bitcast_fusion
  601.3 5.3 fusion
  (21 shorter events, 0.3 us)
Async XLA Ops:
  7.2 204.0 %copy-start = (bf16[1,128,5376]{2,1,0:T(8,128)(2,1)S(1)}, bf16[1,128,5376]{2,1,0:T(8,128)(2,1)}, u32[]{:S(2)}) copy-start(bf16[1,128,5376]{2,1,0:T(8,128)(2,1)} %param.9) | copy-start | bytes 4128772
  35.5 11.2 %copy-start.2 = (bf16[128]{0:T(256)(128)(2,1)S(1)}, bf16[128]{0:T(256)(128)(2,1)}, u32[]{:S(2)}) copy-start(bf16[128]{0:T(256)(128)(2,1)} %param.13) | copy-start | bytes 772
  35.5 169.2 %all-to-all-start = ((bf16[16,40,5376]{2,1,0:T(8,128)(2,1)}), bf16[16,40,5376]{2,1,0:T(8,128)(2,1)}, u32[]{:S(2)}, u32[]{:S(2)}) async-start(bf16[16,40,5376]{2,1,0:T(8,128)(2,1)} %select_select_fusion), calls=%async_computation | async-start | bytes 13762560 | tf_op jit(solution)/shard_map/all_to_all | solution.py:43
  204.7 14.9 %all-to-all-start.3 = ((s32[16,1,40]{2,1,0:T(1,128)}), s32[16,1,40]{2,1,0:T(1,128)S(1)}, u32[]{:S(2)}, u32[]{:S(2)}) async-start(s32[16,1,40]{2,1,0:T(1,128)} %bitcast.12), calls=%async_computation.3 | async-start | bytes 16384 | tf_op jit(solution)/shard_map/all_to_all | solution.py:45
  211.2 50.1 %copy-start.1 = (s32[128]{0:T(128)S(1)}, s32[128]{0:T(128)}, u32[]{:S(2)}) copy-start(s32[128]{0:T(128)} %param.11) | copy-start | bytes 1540
  219.6 13.8 %all-to-all-start.1 = ((f32[16,1,40]{2,1,0:T(1,128)}), f32[16,1,40]{2,1,0:T(1,128)S(1)}, u32[]{:S(2)}, u32[]{:S(2)}) async-start(f32[16,1,40]{2,1,0:T(1,128)} %bitcast.5), calls=%async_computation.1 | async-start | bytes 16384 | tf_op jit(solution)/shard_map/all_to_all | solution.py:56
  233.4 11.9 %all-to-all-start.2 = ((f32[16,1,40]{2,1,0:T(1,128)}), f32[16,1,40]{2,1,0:T(1,128)S(1)}, u32[]{:S(2)}, u32[]{:S(2)}) async-start(f32[16,1,40]{2,1,0:T(1,128)} %bitcast.9), calls=%async_computation.2 | async-start | bytes 16384 | tf_op jit(solution)/shard_map/all_to_all | solution.py:57
  245.3 11.9 %all-to-all-start.4 = ((f32[16,1,40]{2,1,0:T(1,128)}), f32[16,1,40]{2,1,0:T(1,128)S(1)}, u32[]{:S(2)}, u32[]{:S(2)}) async-start(f32[16,1,40]{2,1,0:T(1,128)} %bitcast.15), calls=%async_computation.4 | async-start | bytes 16384 | tf_op jit(solution)/shard_map/all_to_all | solution.py:58
  257.1 11.9 %all-to-all-start.5 = ((bf16[16,1,40]{2,1,0:T(2,128)(2,1)}), bf16[16,1,40]{2,1,0:T(2,128)(2,1)S(1)}, u32[]{:S(2)}, u32[]{:S(2)}) async-start(bf16[16,1,40]{2,1,0:T(2,128)(2,1)} %copy.37), calls=%async_computation.5 | async-start | bytes 16384 | tf_op jit(solution)/shard_map/all_to_all | solution.py:46
  269.0 14.6 %all-to-all-start.6 = ((f32[16,1,40]{2,1,0:T(1,128)}), f32[16,1,40]{2,1,0:T(1,128)S(1)}, u32[]{:S(2)}, u32[]{:S(2)}) async-start(f32[16,1,40]{2,1,0:T(1,128)} %copy_select_fusion), calls=%async_computation.6 | async-start | bytes 16384 | tf_op jit(solution)/shard_map/all_to_all | solution.py:70
  288.5 312.8 %all-to-all-start.7 = ((bf16[16,40,5376]{2,1,0:T(8,128)(2,1)}), bf16[16,40,5376]{2,1,0:T(8,128)(2,1)}, u32[]{:S(2)}, u32[]{:S(2)}) async-start(bf16[16,40,5376]{2,1,0:T(8,128)(2,1)} %convolution_convert_fusion), calls=%async_computation.7 | async-start | bytes 13762560 | tf_op jit(solution)/shard_map/all_to_all | solution.py:78
  293.2 306.5 %all-reduce.3.cloned.1.call-start = ((), (), s32[]{:S(2)}) async-start(), calls=%async_computation.8 | async-start | bytes 5505024
Sparse Core Ops, SparseCore 0:
  299.3 300.3 all-reduce.2
where the time goes:
time: 614 us; the launch traced here: 613 us
  waiting for transfers between devices  490 us (80%)
  starting transfers between devices  44.1 us (7%)
  local copies, waits for them, and re-layouts  26.4 us (4%)
  matrix products  21.9 us (4%)
  other arithmetic  15.9 us (3%)
  between operations  14.9 us (2%)
    unnamed x2, waiting for transfers between devices  299 us
    all_to_all x1, waiting for transfers between devices, shards(): lax.all_to_all(sent_rows, 'vocab', split_axis=0, concat_axis=0, tiled=True)  157 us
    gather x1, local copies, waits for them, and re-layouts, shards(): jnp.take(final_states, slot_row, axis=0)  16.4 us
  transfers between devices with their start and end apart: 9, of which 8 were waited for; matrix products, arithmetic and copies ran while one was open for 4% of the time, Pallas kernels for 0%

commit v1 on v0

v1 whole, which is shorter than its diff:
```python
import jax
import jax.numpy as jnp
from jax import lax
from jax.sharding import Mesh, PartitionSpec as P

LANGS = 4
XH, Y, CORE = 2, 8, 2
Z, XL = 8, 2
DP = ("xh", "y", "core")
VOCAB = ("z", "xl")
F32 = jnp.float32
BF16 = jnp.bfloat16


def swap_all(value, axis):
    return lax.all_to_all(value, axis, split_axis=0, concat_axis=0, tiled=True)


def shards(final_states, head_blocks, block_order, row_tags, target_word, row_weight):
    rows, width = final_states.shape
    blocks = block_order.shape[0]
    words = head_blocks.shape[1]
    short = blocks // LANGS
    feats = width // Y
    wide = -(-feats // 128) * 128
    half_words = words // CORE
    group = rows * Y
    half_cols = short * half_words
    core = lax.axis_index("core")
    y_here = lax.axis_index("y")

    sliced = jnp.transpose(final_states.reshape(rows, Y, feats), (1, 0, 2))
    tag_lanes = jnp.broadcast_to(
        row_tags.astype(BF16)[None, :, None], (Y, rows, wide - feats)
    )
    states = swap_all(jnp.concatenate([sliced, tag_lanes], axis=2), "y").reshape(group, wide)

    own_words = lax.dynamic_index_in_dim(
        head_blocks[0].reshape(XH * Y, CORE, -1, width), core, axis=1, keepdims=False
    ).reshape(half_words, width)
    piece = lax.dynamic_slice_in_dim(own_words, y_here * feats, feats, axis=1)
    piece = jnp.pad(piece, ((0, 0), (0, wide - feats)))
    got_head = swap_all(jnp.broadcast_to(piece[None], (blocks, half_words, wide)), VOCAB)
    own_head = jnp.take(got_head, block_order, axis=0).reshape(blocks * half_words, wide)
    other_head = lax.ppermute(own_head, "core", [(0, 1), (1, 0)])

    tags = states[:, feats].astype(jnp.int32)
    tag_hit = [tags[:, None] == tag for tag in range(LANGS)]

    def pick(all_logits):
        picked = all_logits[:, :half_cols]
        for tag in range(1, LANGS):
            picked = jnp.where(
                tag_hit[tag], all_logits[:, tag * half_cols:(tag + 1) * half_cols], picked
            )
        return picked

    def logits_of(head):
        return pick(
            lax.dot_general(states, head, (((1,), (1,)), ((), ())), preferred_element_type=F32)
        )

    partial = jnp.concatenate([logits_of(own_head), logits_of(other_head)], axis=1)
    logits = jnp.sum(swap_all(partial.reshape(Y, rows, 2 * half_cols), "y"), axis=0)

    slot = target_word // words
    word = target_word % words
    fine = words // (XH * Y * CORE)
    word_core = word // fine % CORE
    word_rank = word // (fine * CORE) * fine + word % fine
    other_half = (word_core != core).astype(jnp.int32)
    position = other_half * half_cols + slot * half_words + word_rank
    target_hit = jnp.arange(2 * half_cols, dtype=jnp.int32)[None, :] == position[:, None]

    peak = jnp.max(logits, axis=1, keepdims=True)
    log_total = peak + jnp.log(jnp.sum(jnp.exp(logits - peak), axis=1, keepdims=True))
    row_loss = log_total[:, 0] - jnp.sum(jnp.where(target_hit, logits, 0.0), axis=1)
    grads = (
        row_weight.astype(F32)[:, None]
        * (jnp.exp(logits - log_total) - target_hit.astype(F32))
    ).astype(BF16)

    all_grads = swap_all(
        jnp.broadcast_to(grads[None], (Y, rows, 2 * half_cols)), "y"
    ).reshape(group, 2 * half_cols)

    def spread(part):
        zero = jnp.zeros((), BF16)
        return jnp.concatenate(
            [jnp.where(tag_hit[tag], part, zero) for tag in range(LANGS)], axis=1
        )

    own_grads = spread(all_grads[:, :half_cols])
    other_grads = spread(all_grads[:, half_cols:])

    def head_term(slot_grads):
        return lax.dot_general(
            slot_grads, states, (((0,), (0,)), ((), ())), preferred_element_type=F32
        )

    passed = lax.ppermute(head_term(other_grads).astype(BF16), "core", [(0, 1), (1, 0)])
    head_sum = (head_term(own_grads) + passed.astype(F32)).astype(BF16)
    block_ids = jnp.arange(blocks, dtype=jnp.int32)
    placed = jnp.sum(
        block_ids[:, None] * (block_order[:, None] == block_ids[None, :]).astype(jnp.int32), axis=0
    )
    by_block = jnp.take(head_sum.reshape(blocks, half_words, wide), placed, axis=0)
    got_terms = jnp.sum(swap_all(by_block, VOCAB).astype(F32), axis=0)[:, :feats]
    shares = swap_all(got_terms.reshape(XH * Y, fine, feats), ("xh", "y"))
    share = jnp.sum(shares.reshape(XH, Y, fine, feats), axis=0)
    head_share = jnp.transpose(share, (1, 0, 2)).reshape(1, fine, width)

    def state_term(slot_grads, head):
        return lax.dot_general(
            slot_grads, head, (((1,), (0,)), ((), ())), preferred_element_type=F32
        )

    state_part = (state_term(own_grads, own_head) + state_term(other_grads, other_head)).astype(BF16)
    state_back = swap_all(state_part.reshape(Y, rows, wide), "y")[:, :, :feats]
    state_grad = jnp.transpose(state_back, (1, 0, 2)).reshape(rows, width)
    return row_loss, state_grad, head_share


def solution(mesh):
    fine_mesh = Mesh(mesh.devices.reshape(XH, Y, CORE, Z, XL), DP + VOCAB)
    every = P(DP + VOCAB)
    return jax.shard_map(
        shards,
        mesh=fine_mesh,
        in_specs=(P(DP + VOCAB, None), P(VOCAB, None, None), P(), every, every, every),
        out_specs=(every, P(DP + VOCAB, None), P(VOCAB, DP, None)),
        check_vma=False,
    )
```

time: 614 us -> 314 us (0.51)
  the two profiles are of different devices: /device:TPU:4 before, /device:TPU:200 now
where the time goes in v1:
time: 314 us; the launch traced here: 313 us
  waiting for transfers between devices  197 us (63%)
  starting transfers between devices  41.4 us (13%)
  blocking collectives  30.4 us (10%)
  matrix products  16.9 us (5%)
  local copies, waits for them, and re-layouts  15.9 us (5%)
  other arithmetic  10.5 us (3%)
    all_to_all x6, waiting for transfers between devices, swap_all(): return lax.all_to_all(value, axis, split_axis=0, concat_axis=0, tiled=True)  193 us
    all_to_all x6, starting transfers between devices, swap_all(): return lax.all_to_all(value, axis, split_axis=0, concat_axis=0, tiled=True)  37.6 us
    all_to_all x1, blocking collectives, swap_all(): return lax.all_to_all(value, axis, split_axis=0, concat_axis=0, tiled=True)  30.4 us
    dot_general x2, matrix products, state_term(): lax.dot_general(slot_grads, head, (((1,), (0,)), ((), ())), preferred_ele...  6.84 us
    dot_general x2, matrix products, logits_of(): lax.dot_general(states, head, (((1,), (1,)), ((), ())), preferred_element...  6.45 us
  transfers between devices with their start and end apart: 8, of which 7 were waited for; matrix products, arithmetic and copies ran while one was open for 8% of the time, Pallas kernels for 0%

profile of v1, /device:TPU:200, one launch (start us, length us, event | category | flops | bytes accessed | tf_op | source)
XLA Modules:
  0.0 312.8 jit_solution(11445958457004986400)
XLA Ops:
  0.6 2.6 reshape_squeeze.3
  3.3 0.2 constant_dynamic-slice_fusion.1
  3.5 0.2 reshape.114
  3.7 0.1 constant_dynamic-slice_fusion
  3.8 1.3 broadcast_in_dim.121
  5.1 9.1 %all-to-all-start.1 = ((bf16[16,64,768]{2,1,0:T(8,128)(2,1)}), bf16[16,64,768]{2,1,0:T(8,128)(2,1)S(1)}, u32[]{:S(2)}, u32[]{:S(2)}) async-start(bf16[16,64,768]{2,1,0:T(8,128)(2,1)} %broadcast_in_dim.121), calls=%async_computation.1 | async-start | bytes 3145728 | tf_op jit(solution)/shard_map/all_to_all | solution.py:16
  14.2 1.8 copy.33
  16.1 1.3 pad_maximum_fusion.2
  17.3 34.5 %all-to-all-done.1 = bf16[16,64,768]{2,1,0:T(8,128)(2,1)S(1)} async-done(((bf16[16,64,768]{2,1,0:T(8,128)(2,1)}), bf16[16,64,768]{2,1,0:T(8,128)(2,1)S(1)}, u32[]{:S(2)}, u32[]{:S(2)}) %all-to-all-start.1) | async-done | bytes 1572896 | tf_op jit(solution)/shard_map/all_to_all | solution.py:16
  51.8 7.5 %all-to-all-start = ((bf16[8,128,768]{1,2,0:T(8,128)(2,1)}), bf16[8,128,768]{1,2,0:T(8,128)(2,1)S(1)}, u32[]{:S(2)}, u32[]{:S(2)}) async-start(bf16[8,128,768]{1,2,0:T(8,128)(2,1)} %pad_maximum_fusion.2), calls=%async_computation | async-start | bytes 3145728 | tf_op jit(solution)/shard_map/all_to_all | solution.py:16
  59.4 1.8 gather_fusion
  61.2 2.8 broadcast_select_fusion.1
  64.0 1.9 collective-permute-start
  65.9 32.1 %all-to-all-done = bf16[8,128,768]{1,2,0:T(8,128)(2,1)S(1)} async-done(((bf16[8,128,768]{1,2,0:T(8,128)(2,1)}), bf16[8,128,768]{1,2,0:T(8,128)(2,1)S(1)}, u32[]{:S(2)}, u32[]{:S(2)}) %all-to-all-start) | async-done | bytes 1572896 | tf_op jit(solution)/shard_map/all_to_all | solution.py:16
  98.0 0.7 copy.34
  98.7 0.7 fusion.7
  99.5 3.2 %fusion.19 = f32[1024,1024]{0,1:T(8,128)S(1)} fusion(bf16[1024,768]{1,0:T(8,128)(2,1)S(1)} %bitcast.36, bf16[1024,768]{1,0:T(8,128)(2,1)} %bitcast.3), kind=kOutput, calls=%fused_computation.80 | convolution fusion | flops 1610612736 | bytes 7340032 | tf_op jit(solution)/shard_map/dot_general | solution.py:60
  102.7 3.2 %fusion.20 = f32[1024,1024]{0,1:T(8,128)S(1)} fusion(bf16[1024,768]{1,0:T(8,128)(2,1)S(1)} %bitcast.37, bf16[1024,768]{1,0:T(8,128)(2,1)} %collective-permute-done), kind=kOutput, calls=%fused_computation.81 | convolution fusion | flops 1610612736 | bytes 7340032 | tf_op jit(solution)/shard_map/dot_general | solution.py:60
  105.9 1.2 fusion.3
  107.1 1.5 copy_bitcast_fusion
  108.6 5.1 %all-to-all-start.2 = ((f32[8,128,512]{1,2,0:T(8,128)}), f32[8,128,512]{1,2,0:T(8,128)S(1)}, u32[]{:S(2)}, u32[]{:S(2)}) async-start(f32[8,128,512]{1,2,0:T(8,128)} %copy_bitcast_fusion), calls=%async_computation.2 | async-start | bytes 4194304 | tf_op jit(solution)/shard_map/all_to_all | solution.py:16
  113.8 50.2 %all-to-all-done.2 = f32[8,128,512]{1,2,0:T(8,128)S(1)} async-done(((f32[8,128,512]{1,2,0:T(8,128)}), f32[8,128,512]{1,2,0:T(8,128)S(1)}, u32[]{:S(2)}, u32[]{:S(2)}) %all-to-all-start.2) | async-done | bytes 2097184 | tf_op jit(solution)/shard_map/all_to_all | solution.py:16
  164.0 0.1 reduce_sum.54
  164.3 0.5 fusion.18
  164.9 0.1 broadcast_in_dim.129
  165.0 30.4 %all_to_all.35 = bf16[8,128,512]{1,2,0:T(8,128)(2,1)S(1)} all-to-all(bf16[8,128,512]{1,2,0:T(8,128)(2,1)S(1)} %broadcast_in_dim.129), channel_id=1, replica_groups=mesh['xh'=2,'y'=8,'core'=2,'z'=8,'xl'=2] {'y'}, dimensions={0} | all-to-all | bytes 2097152 | tf_op jit(solution)/shard_map/all_to_all | solution.py:16
  195.4 0.1 copy_bitcast_fusion.1
  195.6 0.3 broadcast_select_fusion.2
  196.0 1.4 copy-done.1
  197.4 1.8 convolution_convert_fusion
  199.2 1.9 collective-permute-start.1
  201.3 3.3 %collective-permute-done.1 = bf16[1024,768]{1,0:T(8,128)(2,1)S(1)} collective-permute-done((bf16[1024,768]{1,0:T(8,128)(2,1)S(1)}, bf16[1024,768]{1,0:T(8,128)(2,1)S(1)}, u32[]{:S(2)}, u32[]{:S(2)}) %collective-permute-start.1) | collective-permute-done | bytes 1572896 | tf_op jit(solution)/shard_map/ppermute | solution.py:101
  204.5 1.8 add_convert_fusion
  206.3 0.6 gather_fusion.1
  207.0 1.4 broadcast_select_fusion
  208.4 5.4 %all-to-all-start.5 = ((bf16[16,64,768]{2,1,0:T(8,128)(2,1)}), bf16[16,64,768]{2,1,0:T(8,128)(2,1)S(1)}, u32[]{:S(2)}, u32[]{:S(2)}) async-start(bf16[16,64,768]{2,1,0:T(8,128)(2,1)} %broadcast_select_fusion), calls=%async_computation.5 | async-start | bytes 3145728 | tf_op jit(solution)/shard_map/all_to_all | solution.py:16
  213.9 3.6 %fusion.9 = f32[1024,768]{1,0:T(8,128)S(1)} fusion(bf16[1024,768]{1,0:T(8,128)(2,1)} %bitcast.3, bf16[1024,256]{0,1:T(8,128)(2,1)} %copy-done.16, bf16[1024,256]{0,1:T(8,128)(2,1)S(1)} %copy-done.15, bf16[1024,256]{0,1:T(8,128)(2,1)S(1)} %copy-done.13, bf16[1024,256]{0,1:T(8,128)(2,1)S(1)} %copy-done.11), kind=kOutput, calls=%fused_computation.37 | convolution fusion | flops 1619001344 | bytes 6815744 | tf_op jit(solution)/shard_map/dot_general | solution.py:114
  217.6 3.3 %add_convert_fusion.1 = bf16[1024,768]{1,0:T(8,128)(2,1)S(1)} fusion(f32[1024,768]{1,0:T(8,128)S(1)} %fusion.9, bf16[1024,768]{1,0:T(8,128)(2,1)} %collective-permute-done, bf16[1024,256]{0,1:T(8,128)(2,1)S(1)} %copy-done.9, bf16[1024,256]{0,1:T(8,128)(2,1)S(1)} %copy-done.7, bf16[1024,256]{0,1:T(8,128)(2,1)S(1)} %copy-done.5, ...), kind=kOutput, calls=%fused_computation.4 | convolution fusion | flops 1620574208 | bytes 8388608 | tf_op jit(solution)/shard_map/dot_general | solution.py:114
  220.8 1.6 copy.37
  222.4 29.3 %all-to-all-done.5 = bf16[16,64,768]{2,1,0:T(8,128)(2,1)S(1)} async-done(((bf16[16,64,768]{2,1,0:T(8,128)(2,1)}), bf16[16,64,768]{2,1,0:T(8,128)(2,1)S(1)}, u32[]{:S(2)}, u32[]{:S(2)}) %all-to-all-start.5) | async-done | bytes 1572896 | tf_op jit(solution)/shard_map/all_to_all | solution.py:16
  251.8 4.9 %all-to-all-start.4 = ((bf16[8,128,768]{1,2,0:T(8,128)(2,1)}), bf16[8,128,768]{1,2,0:T(8,128)(2,1)S(1)}, u32[]{:S(2)}, u32[]{:S(2)}) async-start(bf16[8,128,768]{1,2,0:T(8,128)(2,1)} %copy.37), calls=%async_computation.4 | async-start | bytes 3145728 | tf_op jit(solution)/shard_map/all_to_all | solution.py:16
  256.7 0.2 convert_reduce_fusion
  256.9 0.7 reshape.121
  257.7 38.0 %all-to-all-done.4 = bf16[8,128,768]{1,2,0:T(8,128)(2,1)S(1)} async-done(((bf16[8,128,768]{1,2,0:T(8,128)(2,1)}), bf16[8,128,768]{1,2,0:T(8,128)(2,1)S(1)}, u32[]{:S(2)}, u32[]{:S(2)}) %all-to-all-start.4) | async-done | bytes 1572896 | tf_op jit(solution)/shard_map/all_to_all | solution.py:16
  295.7 5.5 %all-to-all-start.6 = ((f32[16,4,672]{2,1,0:T(4,128)}), f32[16,4,672]{2,1,0:T(4,128)S(1)}, u32[]{:S(2)}, u32[]{:S(2)}) async-start(f32[16,4,672]{2,1,0:T(4,128)} %reshape.121), calls=%async_computation.6 | async-start | bytes 393216 | tf_op jit(solution)/shard_map/all_to_all | solution.py:16
  301.3 1.5 copy.40
  302.8 9.1 %all-to-all-done.6 = f32[16,4,672]{2,1,0:T(4,128)S(1)} async-done(((f32[16,4,672]{2,1,0:T(4,128)}), f32[16,4,672]{2,1,0:T(4,128)S(1)}, u32[]{:S(2)}, u32[]{:S(2)}) %all-to-all-start.6) | async-done | bytes 172064 | tf_op jit(solution)/shard_map/all_to_all | solution.py:16
  312.0 0.8 reshape.123
  (60 shorter events, 0.7 us)
Async XLA Ops:
  5.1 46.7 %all-to-all-start.1 = ((bf16[16,64,768]{2,1,0:T(8,128)(2,1)}), bf16[16,64,768]{2,1,0:T(8,128)(2,1)S(1)}, u32[]{:S(2)}, u32[]{:S(2)}) async-start(bf16[16,64,768]{2,1,0:T(8,128)(2,1)} %broadcast_in_dim.121), calls=%async_computation.1 | async-start | bytes 3145728 | tf_op jit(solution)/shard_map/all_to_all | solution.py:16
  14.2 1.8 copy-start.17
  17.3 42.0 %copy-start.20 = (s32[16]{0:T(128)S(1)}, s32[16]{0:T(128)}, u32[]{:S(2)}) copy-start(s32[16]{0:T(128)} %param.10) | copy-start | bytes 196
  51.8 46.2 %all-to-all-start = ((bf16[8,128,768]{1,2,0:T(8,128)(2,1)}), bf16[8,128,768]{1,2,0:T(8,128)(2,1)S(1)}, u32[]{:S(2)}, u32[]{:S(2)}) async-start(bf16[8,128,768]{1,2,0:T(8,128)(2,1)} %pad_maximum_fusion.2), calls=%async_computation | async-start | bytes 3145728 | tf_op jit(solution)/shard_map/all_to_all | solution.py:16
  64.0 38.7 %collective-permute-start = (bf16[1024,768]{1,0:T(8,128)(2,1)}, bf16[1024,768]{1,0:T(8,128)(2,1)}, u32[]{:S(2)}, u32[]{:S(2)}) collective-permute-start(bf16[1024,768]{1,0:T(8,128)(2,1)} %bitcast.3), channel_id=1, source_target_pairs={{0,16},{16,0},{1,17},{17,1},{2,18},{18,2},{3,19},{19,3},{4,20},{20... | collective-permute-start | bytes 4718600 | tf_op jit(solution)/shard_map/ppermute | solution.py:45
  98.7 4.0 %copy-start = (bf16[8,128,768]{2,1,0:T(8,128)(2,1)}, bf16[8,128,768]{2,1,0:T(8,128)(2,1)S(1)}, u32[]{:S(2)}) copy-start(bf16[8,128,768]{2,1,0:T(8,128)(2,1)S(1)} %copy.34) | copy-start | bytes 4718596
  108.6 5.1 %copy-start.18 = (bf16[128]{0:T(256)(128)(2,1)S(1)}, bf16[128]{0:T(256)(128)(2,1)}, u32[]{:S(2)}) copy-start(bf16[128]{0:T(256)(128)(2,1)} %param.13) | copy-start | bytes 772
  108.6 5.1 %copy-start.19 = (s32[128]{0:T(128)S(1)}, s32[128]{0:T(128)}, u32[]{:S(2)}) copy-start(s32[128]{0:T(128)} %param.12) | copy-start | bytes 1540
  108.6 55.3 %all-to-all-start.2 = ((f32[8,128,512]{1,2,0:T(8,128)}), f32[8,128,512]{1,2,0:T(8,128)S(1)}, u32[]{:S(2)}, u32[]{:S(2)}) async-start(f32[8,128,512]{1,2,0:T(8,128)} %copy_bitcast_fusion), calls=%async_computation.2 | async-start | bytes 4194304 | tf_op jit(solution)/shard_map/all_to_all | solution.py:16
  195.6 1.8 copy-start.1
  195.9 3.3 %copy-start.2 = (bf16[1024,256]{0,1:T(8,128)(2,1)}, bf16[1024,256]{0,1:T(8,128)(2,1)S(1)}, u32[]{:S(2)}) copy-start(bf16[1024,256]{0,1:T(8,128)(2,1)S(1)} %get-tuple-element.27) | copy-start | bytes 1572868
  195.9 3.3 %copy-start.4 = (bf16[1024,256]{0,1:T(8,128)(2,1)}, bf16[1024,256]{0,1:T(8,128)(2,1)S(1)}, u32[]{:S(2)}) copy-start(bf16[1024,256]{0,1:T(8,128)(2,1)S(1)} %get-tuple-element.36) | copy-start | bytes 1572868
  195.9 3.3 %copy-start.6 = (bf16[1024,256]{0,1:T(8,128)(2,1)}, bf16[1024,256]{0,1:T(8,128)(2,1)S(1)}, u32[]{:S(2)}) copy-start(bf16[1024,256]{0,1:T(8,128)(2,1)S(1)} %get-tuple-element.38) | copy-start | bytes 1572868
  195.9 3.3 %copy-start.8 = (bf16[1024,256]{0,1:T(8,128)(2,1)}, bf16[1024,256]{0,1:T(8,128)(2,1)S(1)}, u32[]{:S(2)}) copy-start(bf16[1024,256]{0,1:T(8,128)(2,1)S(1)} %get-tuple-element.40) | copy-start | bytes 1572868
  195.9 8.6 %copy-start.10 = (bf16[1024,256]{0,1:T(8,128)(2,1)}, bf16[1024,256]{0,1:T(8,128)(2,1)S(1)}, u32[]{:S(2)}) copy-start(bf16[1024,256]{0,1:T(8,128)(2,1)S(1)} %get-tuple-element.28) | copy-start | bytes 1572868
  195.9 8.6 %copy-start.12 = (bf16[1024,256]{0,1:T(8,128)(2,1)}, bf16[1024,256]{0,1:T(8,128)(2,1)S(1)}, u32[]{:S(2)}) copy-start(bf16[1024,256]{0,1:T(8,128)(2,1)S(1)} %get-tuple-element.35) | copy-start | bytes 1572868
  195.9 8.6 %copy-start.14 = (bf16[1024,256]{0,1:T(8,128)(2,1)}, bf16[1024,256]{0,1:T(8,128)(2,1)S(1)}, u32[]{:S(2)}) copy-start(bf16[1024,256]{0,1:T(8,128)(2,1)S(1)} %get-tuple-element.37) | copy-start | bytes 1572868
  195.9 8.6 %copy-start.16 = (bf16[1024,256]{0,1:T(8,128)(2,1)}, bf16[1024,256]{0,1:T(8,128)(2,1)S(1)}, u32[]{:S(2)}) copy-start(bf16[1024,256]{0,1:T(8,128)(2,1)S(1)} %get-tuple-element.39) | copy-start | bytes 1572868
  199.2 5.3 %collective-permute-start.1 = (bf16[1024,768]{1,0:T(8,128)(2,1)S(1)}, bf16[1024,768]{1,0:T(8,128)(2,1)S(1)}, u32[]{:S(2)}, u32[]{:S(2)}) collective-permute-start(bf16[1024,768]{1,0:T(8,128)(2,1)S(1)} %convolution_convert_fusion), channel_id=1, source_target_pairs={{0,16},{16,0},{1,17},{17,1},{2,18},{18,2},{3,19},{19,3},{4,20},{20... | collective-permute-start | bytes 4718600 | tf_op jit(solution)/shard_map/ppermute | solution.py:101
  208.4 5.4 %copy-start.11 = (bf16[1024,256]{0,1:T(8,128)(2,1)S(1)}, bf16[1024,256]{0,1:T(8,128)(2,1)}, u32[]{:S(2)}) copy-start(bf16[1024,256]{0,1:T(8,128)(2,1)} %copy-done.10) | copy-start | bytes 1572868
  208.4 5.4 %copy-start.13 = (bf16[1024,256]{0,1:T(8,128)(2,1)S(1)}, bf16[1024,256]{0,1:T(8,128)(2,1)}, u32[]{:S(2)}) copy-start(bf16[1024,256]{0,1:T(8,128)(2,1)} %copy-done.12) | copy-start | bytes 1572868
  208.4 5.4 %copy-start.15 = (bf16[1024,256]{0,1:T(8,128)(2,1)S(1)}, bf16[1024,256]{0,1:T(8,128)(2,1)}, u32[]{:S(2)}) copy-start(bf16[1024,256]{0,1:T(8,128)(2,1)} %copy-done.14) | copy-start | bytes 1572868
  208.4 43.3 %all-to-all-start.5 = ((bf16[16,64,768]{2,1,0:T(8,128)(2,1)}), bf16[16,64,768]{2,1,0:T(8,128)(2,1)S(1)}, u32[]{:S(2)}, u32[]{:S(2)}) async-start(bf16[16,64,768]{2,1,0:T(8,128)(2,1)} %broadcast_select_fusion), calls=%async_computation.5 | async-start | bytes 3145728 | tf_op jit(solution)/shard_map/all_to_all | solution.py:16
  213.9 3.6 %copy-start.3 = (bf16[1024,256]{0,1:T(8,128)(2,1)S(1)}, bf16[1024,256]{0,1:T(8,128)(2,1)}, u32[]{:S(2)}) copy-start(bf16[1024,256]{0,1:T(8,128)(2,1)} %copy-done.2) | copy-start | bytes 1572868
  213.9 3.6 %copy-start.5 = (bf16[1024,256]{0,1:T(8,128)(2,1)S(1)}, bf16[1024,256]{0,1:T(8,128)(2,1)}, u32[]{:S(2)}) copy-start(bf16[1024,256]{0,1:T(8,128)(2,1)} %copy-done.4) | copy-start | bytes 1572868
  213.9 3.6 %copy-start.7 = (bf16[1024,256]{0,1:T(8,128)(2,1)S(1)}, bf16[1024,256]{0,1:T(8,128)(2,1)}, u32[]{:S(2)}) copy-start(bf16[1024,256]{0,1:T(8,128)(2,1)} %copy-done.6) | copy-start | bytes 1572868
  213.9 3.6 %copy-start.9 = (bf16[1024,256]{0,1:T(8,128)(2,1)S(1)}, bf16[1024,256]{0,1:T(8,128)(2,1)}, u32[]{:S(2)}) copy-start(bf16[1024,256]{0,1:T(8,128)(2,1)} %copy-done.8) | copy-start | bytes 1572868
  251.8 43.9 %all-to-all-start.4 = ((bf16[8,128,768]{1,2,0:T(8,128)(2,1)}), bf16[8,128,768]{1,2,0:T(8,128)(2,1)S(1)}, u32[]{:S(2)}, u32[]{:S(2)}) async-start(bf16[8,128,768]{1,2,0:T(8,128)(2,1)} %copy.37), calls=%async_computation.4 | async-start | bytes 3145728 | tf_op jit(solution)/shard_map/all_to_all | solution.py:16
  295.7 16.2 %all-to-all-start.6 = ((f32[16,4,672]{2,1,0:T(4,128)}), f32[16,4,672]{2,1,0:T(4,128)S(1)}, u32[]{:S(2)}, u32[]{:S(2)}) async-start(f32[16,4,672]{2,1,0:T(4,128)} %reshape.121), calls=%async_computation.6 | async-start | bytes 393216 | tf_op jit(solution)/shard_map/all_to_all | solution.py:16
